TPU v7x, 32 devices: a whole 2x2x4 slice. The times are simulated.
32 devices in a mesh: wide: 8 (over z, x), narrow: 4 (over y, core).
Axes of the slice: x: 2, y: 2, z: 4, core: 2. Of those that a mesh axis runs over, the one named last changes fastest.
Arguments:
- tokens: bfloat16 [16, 1024, 768], P('wide', 'narrow'), may hold values from -6 to 6
- segment_ids: int32 [16, 1024], P('wide'), may hold values from -1 to 7, as said below
- cotangent: bfloat16 [16, 1024, 768], P('wide', 'narrow'), may hold values from -6 to 6
- attn_w: float32 [4, 768, 768], P(None, 'wide', 'narrow')
- attn_m: float32 [4, 768, 768], P(None, 'wide', 'narrow')
- attn_v: float32 [4, 768, 768], P(None, 'wide', 'narrow')
- mlp_w: float32 [2, 768, 3072], P(None, 'wide', 'narrow')
- mlp_m: float32 [2, 768, 3072], P(None, 'wide', 'narrow')
- mlp_v: float32 [2, 768, 3072], P(None, 'wide', 'narrow')
- vectors: float32 [12, 768], replicated
- vec_m: float32 [12, 768], replicated
- vec_v: float32 [12, 768], replicated
Outputs:
- block_out: bfloat16 [16, 1024, 768], P('wide', 'narrow')
- block_input_gradient: float32 [16, 1024, 768], P('wide', 'narrow')
- attn_grad: float32 [4, 768, 768], P(None, 'wide', 'narrow')
- attn_new: float32 [4, 768, 768], P(None, 'wide', 'narrow')
- attn_m_new: float32 [4, 768, 768], P(None, 'wide', 'narrow')
- attn_v_new: float32 [4, 768, 768], P(None, 'wide', 'narrow')
- mlp_grad: float32 [2, 768, 3072], P(None, 'wide', 'narrow')
- mlp_new: float32 [2, 768, 3072], P(None, 'wide', 'narrow')
- mlp_m_new: float32 [2, 768, 3072], P(None, 'wide', 'narrow')
- mlp_v_new: float32 [2, 768, 3072], P(None, 'wide', 'narrow')
- vec_grad: float32 [12, 768], replicated
- vec_new: float32 [12, 768], replicated
- vec_m_new: float32 [12, 768], replicated
- vec_v_new: float32 [12, 768], replicated
Inputs may be any that keep to these rules, and one draw needn't show every extreme that they name: `segment_ids`: in each row the ids start at 0, never fall along the slots and are at most 7; the last slots of a row (at most 51) hold -1 for padding.
All inputs are finite; a program needn't handle non-finite values.
Results may differ from a plain program's by a relative error of at most 0.019.
Values may be sent and summed in bfloat16 or wider, within the bound.
No kernel may reach another device: no remote copies, remote signals or barrier semaphores. Data moves between devices by JAX's collectives and lax.ppermute only.
A program may use at most 128 MiB of HBM per device.

v0:
```python
import jax
import jax.numpy as jnp
from jax import lax
from jax.sharding import PartitionSpec as P

HEAD_DIM = 64
STEP = 10
EPS_NORM = 1e-06
MASKED_SCORE = -1e30
BETA_ONE = 0.5
BETA_TWO = 0.5
EPS_ADAM = 1e-08
RATE_MATRIX = 0.04
RATE_VECTOR = 0.3
DECAY_MATRIX = 0.05


def norm_shard_pieces(values_in, gain_vec, shift_vec):
    row_mean = jnp.mean(values_in, axis=-1, keepdims=True)
    centred = values_in - row_mean
    row_var = jnp.mean(centred * centred, axis=-1, keepdims=True)
    inv_std = lax.rsqrt(row_var + EPS_NORM)
    normed = centred * inv_std
    return (normed * gain_vec + shift_vec, normed, inv_std)


def norm_backward_pass(grad_out, normed, inv_std, gain_vec):
    scaled = grad_out * gain_vec
    return inv_std * (
        scaled
        - jnp.mean(scaled, axis=-1, keepdims=True)
        - normed * jnp.mean(scaled * normed, axis=-1, keepdims=True)
    )


def exact_gelu(values_in):
    return jax.nn.gelu(values_in, approximate=False)


def local_shard_portion(rows_in, sequence_count, start, count):
    shaped = rows_in.reshape(sequence_count, -1, rows_in.shape[-1])
    return lax.dynamic_slice_in_dim(shaped, start, count, 1)


def adamw_update(weight, first_mom, second, gradient, step_rate, decay_rate):
    first_new = BETA_ONE * first_mom + (1.0 - BETA_ONE) * gradient
    second_new = BETA_TWO * second + (1.0 - BETA_TWO) * gradient * gradient
    corrected = (
        first_new
        / (1.0 - BETA_ONE**STEP)
        / (jnp.sqrt(second_new / (1.0 - BETA_TWO**STEP)) + EPS_ADAM)
    )
    return (weight - step_rate * (corrected + decay_rate * weight), first_new, second_new)


def local(
    tokens,
    segment_ids,
    cotangent,
    attn_w,
    attn_m,
    attn_v,
    mlp_w,
    mlp_m,
    mlp_v,
    vectors,
    vec_m,
    vec_v,
):
    narrow_count = lax.axis_size("narrow")
    narrow_index = lax.axis_index("narrow")
    sequence_count, shard_length, width = tokens.shape
    seq_len = segment_ids.shape[1]
    token_count = sequence_count * seq_len
    local_cols = attn_w.shape[2]
    local_hidden = mlp_w.shape[2]
    head_local = local_cols // HEAD_DIM
    block_len = min(seq_len, 512)
    block_count = seq_len // block_len
    scale = HEAD_DIM ** (-0.5)
    shard_offset = narrow_index * shard_length
    attn_full, mlp_full = (
        lax.all_gather(attn_w.astype(jnp.bfloat16), "wide", axis=1, tiled=True),
        lax.all_gather(mlp_w.astype(jnp.bfloat16), "wide", axis=1, tiled=True),
    )
    tokens_all, cot_all = (
        lax.all_gather(tokens, "narrow", axis=1, tiled=True),
        lax.all_gather(cotangent, "narrow", axis=1, tiled=True),
    )
    input_tokens = tokens_all.reshape(token_count, width).astype(jnp.float32)
    cotangent_token_rows = cot_all.reshape(token_count, width)
    own_inputs = tokens.astype(jnp.float32)
    own_cot = cotangent.astype(jnp.float32)
    first_norm_gain = vectors[0]
    first_norm_bias = vectors[1]
    second_norm_gain = vectors[2]
    second_norm_bias = vectors[3]
    out_bias = vectors[4]
    down_bias = vectors[5]
    query_bias = lax.dynamic_slice_in_dim(vectors[6], narrow_index * local_cols, local_cols)
    value_bias = lax.dynamic_slice_in_dim(vectors[7], narrow_index * local_cols, local_cols)
    up_bias = lax.dynamic_slice_in_dim(
        vectors[8:].reshape(-1), narrow_index * local_hidden, local_hidden
    )
    normalized_input, first_standardized, first_inverse_std = norm_shard_pieces(
        input_tokens, first_norm_gain, first_norm_bias
    )
    norm_low = normalized_input.astype(jnp.bfloat16)
    projected = jnp.einsum(
        "td,cde->cte", norm_low, attn_full[:3], preferred_element_type=jnp.float32
    )
    col_bias = jnp.stack([query_bias, jnp.zeros_like(query_bias), value_bias])
    qkv_low = (projected + col_bias[:, None, :]).astype(jnp.bfloat16)
    queries = qkv_low[0].reshape(sequence_count, seq_len, head_local, HEAD_DIM)
    key_rows = qkv_low[1].reshape(sequence_count, seq_len, head_local, HEAD_DIM)
    value_rows = qkv_low[2].reshape(sequence_count, seq_len, head_local, HEAD_DIM)

    def scores_for(block_index):
        row_index = block_index // block_count
        start = block_index % block_count * block_len
        query_block = lax.dynamic_slice_in_dim(
            lax.dynamic_index_in_dim(queries, row_index, 0, False), start, block_len, 0
        )
        key_block = lax.dynamic_index_in_dim(key_rows, row_index, 0, False)
        value_block = lax.dynamic_index_in_dim(value_rows, row_index, 0, False)
        seg_row = lax.dynamic_index_in_dim(segment_ids, row_index, 0, False)
        seg_query = lax.dynamic_slice_in_dim(seg_row, start, block_len, 0)
        raw = (
            jnp.einsum("qhd,khd->hqk", query_block, key_block, preferred_element_type=jnp.float32)
            * scale
        )
        same_doc = seg_query[:, None] == seg_row[None, :]
        masked = jnp.where(same_doc[None], raw, MASKED_SCORE)
        return (masked, query_block, key_block, value_block, row_index, start)

    def attend(block_index):
        masked, query_block, key_block, value_block, row_index, start = scores_for(block_index)
        top_score = jnp.max(masked, axis=-1, keepdims=True)
        expo = jnp.exp(masked - top_score)
        total = jnp.sum(expo, axis=-1, keepdims=True)
        probs_low = (expo / total).astype(jnp.bfloat16)
        context = jnp.einsum(
            "hqk,khd->qhd", probs_low, value_block, preferred_element_type=jnp.float32
        ).astype(jnp.bfloat16)
        return (context, top_score[..., 0] + jnp.log(total[..., 0]))

    block_ids = jnp.arange(sequence_count * block_count)
    contexts, log_totals = lax.map(attend, block_ids)
    context_rows = contexts.reshape(token_count, local_cols)
    out_part = jnp.einsum(
        "tc,dc->td", context_rows, attn_full[3], preferred_element_type=jnp.float32
    )
    out_share = lax.psum_scatter(
        out_part.reshape(sequence_count, seq_len, width), "narrow", scatter_dimension=1, tiled=True
    )
    hidden_own = own_inputs + out_share + out_bias
    normed_two_own, second_standardized_local, inv_two_own = norm_shard_pieces(
        hidden_own, second_norm_gain, second_norm_bias
    )
    second_in = lax.all_gather(
        normed_two_own.astype(jnp.bfloat16), "narrow", axis=1, tiled=True
    ).reshape(token_count, width)
    pre_act = jnp.dot(second_in, mlp_full[0], preferred_element_type=jnp.float32) + up_bias
    activated = exact_gelu(pre_act).astype(jnp.bfloat16)
    down_part = jnp.einsum("tf,df->td", activated, mlp_full[1], preferred_element_type=jnp.float32)
    down_share = lax.psum_scatter(
        down_part.reshape(sequence_count, seq_len, width).astype(jnp.bfloat16),
        "narrow",
        scatter_dimension=1,
        tiled=True,
    ).astype(jnp.float32)
    block_own = hidden_own + down_share + down_bias
    block_out = block_own.astype(jnp.bfloat16)
    grad_down_w = jnp.einsum(
        "td,tf->df", cotangent_token_rows, activated, preferred_element_type=jnp.float32
    )
    grad_act = jnp.dot(cotangent_token_rows, mlp_full[1], preferred_element_type=jnp.float32)
    unused_value, gelu_pull = jax.vjp(exact_gelu, pre_act)
    grad_pre = gelu_pull(grad_act)[0].astype(jnp.bfloat16)
    grad_up_w = jnp.einsum("td,tf->df", second_in, grad_pre, preferred_element_type=jnp.float32)
    grad_up_bias = jnp.sum(grad_pre, axis=0, dtype=jnp.float32)
    norm_two_part = jnp.einsum(
        "tf,df->td", grad_pre, mlp_full[0], preferred_element_type=jnp.float32
    )
    second_norm_local = lax.psum_scatter(
        norm_two_part.reshape(sequence_count, seq_len, width),
        "narrow",
        scatter_dimension=1,
        tiled=True,
    )
    residual_local = own_cot + norm_backward_pass(
        second_norm_local, second_standardized_local, inv_two_own, second_norm_gain
    )
    resid_low = lax.all_gather(
        residual_local.astype(jnp.bfloat16), "narrow", axis=1, tiled=True
    ).reshape(token_count, width)
    grad_out_w = jnp.einsum(
        "td,tc->dc", resid_low, context_rows, preferred_element_type=jnp.float32
    )
    grad_context = jnp.dot(resid_low, attn_full[3], preferred_element_type=jnp.float32).astype(
        jnp.bfloat16
    )
    grad_context = grad_context.reshape(sequence_count, seq_len, head_local, HEAD_DIM)

    def attend_back(block_index):
        masked, query_block, key_block, value_block, row_index, start = scores_for(block_index)
        grad_block = lax.dynamic_slice_in_dim(
            lax.dynamic_index_in_dim(grad_context, row_index, 0, False), start, block_len, 0
        )
        log_block = lax.dynamic_index_in_dim(log_totals, block_index, 0, False)
        probs = jnp.exp(masked - log_block[..., None])
        probs_low = probs.astype(jnp.bfloat16)
        grad_values = jnp.einsum(
            "hqk,qhd->khd", probs_low, grad_block, preferred_element_type=jnp.float32
        )
        grad_probs = jnp.einsum(
            "qhd,khd->hqk", grad_block, value_block, preferred_element_type=jnp.float32
        )
        inner = jnp.sum(probs * grad_probs, axis=-1, keepdims=True)
        grad_scores = (probs * (grad_probs - inner)).astype(jnp.bfloat16)
        grad_query = (
            jnp.einsum("hqk,khd->qhd", grad_scores, key_block, preferred_element_type=jnp.float32)
            * scale
        )
        grad_keys = (
            jnp.einsum("hqk,qhd->khd", grad_scores, query_block, preferred_element_type=jnp.float32)
            * scale
        )
        return (grad_query, grad_keys, grad_values)

    query_parts, key_parts, value_parts = lax.map(attend_back, block_ids)
    grad_query_rows = query_parts.reshape(token_count, local_cols)
    grad_key_rows = (
        key_parts.reshape(sequence_count, block_count, seq_len, local_cols)
        .sum(axis=1)
        .reshape(token_count, local_cols)
    )
    grad_value_rows = (
        value_parts.reshape(sequence_count, block_count, seq_len, local_cols)
        .sum(axis=1)
        .reshape(token_count, local_cols)
    )
    grad_qkv = jnp.stack([grad_query_rows, grad_key_rows, grad_value_rows]).astype(jnp.bfloat16)
    grad_qkv_w = jnp.einsum("td,cte->cde", norm_low, grad_qkv, preferred_element_type=jnp.float32)
    grad_query_bias = jnp.sum(grad_qkv[0], axis=0, dtype=jnp.float32)
    grad_value_bias = jnp.sum(grad_qkv[2], axis=0, dtype=jnp.float32)
    norm_one_part = jnp.einsum(
        "cte,cde->td", grad_qkv, attn_full[:3], preferred_element_type=jnp.float32
    )
    first_norm_local = lax.psum_scatter(
        norm_one_part.reshape(sequence_count, seq_len, width).astype(jnp.bfloat16),
        "narrow",
        scatter_dimension=1,
        tiled=True,
    ).astype(jnp.float32)
    first_standardized_local = local_shard_portion(
        first_standardized, sequence_count, shard_offset, shard_length
    )
    first_inverse_std_local = local_shard_portion(
        first_inverse_std, sequence_count, shard_offset, shard_length
    )
    block_input_gradient = residual_local + norm_backward_pass(
        first_norm_local, first_standardized_local, first_inverse_std_local, first_norm_gain
    )
    fixed_rows = jnp.stack(
        [
            jnp.sum(first_norm_local * first_standardized_local, axis=(0, 1)),
            jnp.sum(first_norm_local, axis=(0, 1)),
            jnp.sum(second_norm_local * second_standardized_local, axis=(0, 1)),
            jnp.sum(second_norm_local, axis=(0, 1)),
            jnp.sum(residual_local, axis=(0, 1)),
            jnp.sum(own_cot, axis=(0, 1)),
        ]
    )
    head_rows = lax.dynamic_update_slice_in_dim(
        jnp.zeros((2, width), jnp.float32),
        jnp.stack([grad_query_bias, grad_value_bias]),
        narrow_index * local_cols,
        1,
    )
    up_rows = lax.dynamic_update_slice_in_dim(
        jnp.zeros((local_hidden * narrow_count,), jnp.float32),
        grad_up_bias,
        narrow_index * local_hidden,
        0,
    ).reshape(-1, width)
    vec_local = jnp.concatenate([fixed_rows, head_rows, up_rows], axis=0)
    vec_grad = lax.psum(vec_local, ("wide", "narrow"))
    attn_local = jnp.concatenate([grad_qkv_w, grad_out_w[None]], axis=0)
    mlp_local = jnp.stack([grad_up_w, grad_down_w])
    attn_grad, mlp_grad = (
        lax.psum_scatter(
            attn_local.astype(jnp.bfloat16), "wide", scatter_dimension=1, tiled=True
        ).astype(jnp.float32),
        lax.psum_scatter(
            mlp_local.astype(jnp.bfloat16), "wide", scatter_dimension=1, tiled=True
        ).astype(jnp.float32),
    )
    attn_new, attn_m_new, attn_v_new = adamw_update(
        attn_w, attn_m, attn_v, attn_grad, RATE_MATRIX, DECAY_MATRIX
    )
    mlp_new, mlp_m_new, mlp_v_new = adamw_update(
        mlp_w, mlp_m, mlp_v, mlp_grad, RATE_MATRIX, DECAY_MATRIX
    )
    vec_new, vec_m_new, vec_v_new = adamw_update(vectors, vec_m, vec_v, vec_grad, RATE_VECTOR, 0.0)
    return (
        block_out,
        block_input_gradient,
        attn_grad,
        attn_new,
        attn_m_new,
        attn_v_new,
        mlp_grad,
        mlp_new,
        mlp_m_new,
        mlp_v_new,
        vec_grad,
        vec_new,
        vec_m_new,
        vec_v_new,
    )


def solution(mesh):
    in_specs = (
        P("wide", "narrow", None),
        P("wide", None),
        P("wide", "narrow", None),
        P(None, "wide", "narrow"),
        P(None, "wide", "narrow"),
        P(None, "wide", "narrow"),
        P(None, "wide", "narrow"),
        P(None, "wide", "narrow"),
        P(None, "wide", "narrow"),
        P(),
        P(),
        P(),
    )
    out_specs = (
        P("wide", "narrow", None),
        P("wide", "narrow", None),
        P(None, "wide", "narrow"),
        P(None, "wide", "narrow"),
        P(None, "wide", "narrow"),
        P(None, "wide", "narrow"),
        P(None, "wide", "narrow"),
        P(None, "wide", "narrow"),
        P(None, "wide", "narrow"),
        P(None, "wide", "narrow"),
        P(),
        P(),
        P(),
        P(),
    )
    return jax.shard_map(local, mesh=mesh, in_specs=in_specs, out_specs=out_specs, check_vma=False)
```

profile of v0, /device:TPU:0, one launch (start us, length us, event | category | flops | bytes accessed | tf_op | source)
XLA Modules:
  0.0 722.1 jit_solution(8954707669613405270)
XLA Ops:
  11.9 45.8 %all-gather.9.cloned.1.call-done = bf16[4,768,192]{2,0,1:T(4,128)(2,1)} async-done(((bf16[4,96,192]{2,0,1:T(4,128)(2,1)}), bf16[4,768,192]{2,0,1:T(4,128)(2,1)}) %all-gather.9.cloned.1.call-update) | async-done | bytes 1179664 | tf_op jit(solution)/shard_map/all_gather | solution.py:83
  61.5 25.1 %all-gather.7.cloned.1.call-done = bf16[2,1024,768]{2,1,0:T(8,128)(2,1)} async-done(((bf16[2,256,768]{2,1,0:T(8,128)(2,1)}), bf16[2,1024,768]{2,1,0:T(8,128)(2,1)}) %all-gather.7.cloned.1.call-update) | async-done | bytes 3145744 | tf_op jit(solution)/shard_map/all_gather | solution.py:87
  89.5 3.8 convert_subtract_fusion
  100.1 39.2 %while.32 = (s32[]{:T(128)}, bf16[4,512,3,64]{1,3,2,0:T(8,128)(2,1)}, f32[4,3,512]{2,1,0:T(4,128)S(1)}, s32[4]{0:T(128)S(1)}, bf16[2,1024,3,64]{1,3,2,0:T(8,128)...) while((s32[]{:T(128)}, ...), condition=%wide.region_5.6_spmd, body=%wide.region_2.5_spmd.sunk | while | flops 422148640 | bytes 22229476 | solution.py:148
  107.1 2.7 fusion.152
  126.5 2.7 fusion.152
  142.8 4.8 fusion.97
  149.5 56.7 %reduce-scatter.9.cloned.1.call-done = f32[2,256,768]{2,1,0:T(8,128)} async-done(((f32[2,1024,768]{2,1,0:T(8,128)}), f32[2,256,768]{2,1,0:T(8,128)}) %reduce-scatter.9.cloned.1.call-update) | async-done | bytes 1572880 | tf_op jit(solution)/shard_map/reduce_scatter | solution.py:153
  210.3 50.6 %all-gather.13.cloned.1.call-done = bf16[2,768,768]{2,1,0:T(8,128)(2,1)} async-done(((bf16[2,96,768]{2,1,0:T(8,128)(2,1)}), bf16[2,768,768]{2,1,0:T(8,128)(2,1)}) %all-gather.13.cloned.1.call-update) | async-done | bytes 2359312 | tf_op jit(solution)/shard_map/all_gather | solution.py:84
  261.0 29.2 %all-gather.11.cloned.1.call-done = bf16[2,1024,768]{2,1,0:T(8,128)(2,1)} async-done(((bf16[2,256,768]{2,1,0:T(8,128)(2,1)}), bf16[2,1024,768]{2,1,0:T(8,128)(2,1)}) %all-gather.11.cloned.1.call-update) | async-done | bytes 3145744 | tf_op jit(solution)/shard_map/all_gather | solution.py:160
  290.1 19.0 %multiply_convert_fusion.1 = (bf16[2048,768]{1,0:T(8,128)(2,1)}, f32[2048,768]{1,0:T(8,128)}, f32[2048,768]{1,0:T(8,128)}) fusion(f32[768]{0:T(1024)S(1)} %dynamic_slice.110, bf16[2048,768]{1,0:T(8,128)(2,1)} %bitcast.256, bf16[2,768,768]{2,1,0:T(8,128)(2,1)} %all-gather.13.cloned.1.call-done), kind=kOutput, calls=%fused_computation.73 | convolution fusion | flops 2519728128 | bytes 20057088 | tf_op jit(solution)/shard_map/dot_general | solution.py:163
  309.1 11.1 %all-gather.15.cloned.1.call-done = bf16[2,1024,768]{2,1,0:T(8,128)(2,1)} async-done(((bf16[2,256,768]{2,1,0:T(8,128)(2,1)}), bf16[2,1024,768]{2,1,0:T(8,128)(2,1)}) %all-gather.15.cloned.1.call-update) | async-done | bytes 3145744 | tf_op jit(solution)/shard_map/all_gather | solution.py:88
  320.2 10.6 %convert_reduce_fusion = (f32[768]{0:T(1024)S(1)}, bf16[2048,768]{1,0:T(8,128)(2,1)S(1)}) fusion(f32[2048,768]{1,0:T(8,128)} %get-tuple-element.504, bf16[2048,768]{1,0:T(8,128)(2,1)} %bitcast.258, bf16[2,768,768]{2,1,0:T(8,128)(2,1)} %all-gather.13.cloned.1.call-done, f32[2048,768]{1,0:T(8,128)} %get-tuple-element.530, f32[768]{0:T(1024)S(1)} %dynamic_slice.110), kind=kOutput, calls=%fused_computation.71 | convolution fusion | flops 2442657024 | bytes 20060160 | tf_op jit(solution)/shard_map/dot_general | solution.py:177
  332.5 4.5 fusion.83
  337.0 6.6 convolution_convert_fusion.1
  343.9 51.6 %reduce-scatter.13.cloned.1.call-done = f32[2,256,768]{2,1,0:T(8,128)} async-done(((f32[2,1024,768]{2,1,0:T(8,128)}), f32[2,256,768]{2,1,0:T(8,128)}) %reduce-scatter.13.cloned.1.call-update) | async-done | bytes 1572880 | tf_op jit(solution)/shard_map/reduce_scatter | solution.py:185
  397.6 38.4 %reduce-scatter.11.cloned.1.call-done = bf16[2,256,768]{2,1,0:T(8,128)(2,1)} async-done(((bf16[2,1024,768]{2,1,0:T(8,128)(2,1)}), bf16[2,256,768]{2,1,0:T(8,128)(2,1)}) %reduce-scatter.11.cloned.1.call-update) | async-done | bytes 786448 | tf_op jit(solution)/shard_map/reduce_scatter | solution.py:166
  436.1 3.6 fusion.107
  442.9 5.6 fusion.79
  453.0 17.5 %all-gather.17.cloned.1.call-done = bf16[2,1024,768]{2,1,0:T(8,128)(2,1)} async-done(((bf16[2,256,768]{2,1,0:T(8,128)(2,1)}), bf16[2,1024,768]{2,1,0:T(8,128)(2,1)}) %all-gather.17.cloned.1.call-update) | async-done | bytes 3145744 | tf_op jit(solution)/shard_map/all_gather | solution.py:194
  470.5 3.1 convolution_convert_fusion
  476.4 64.6 %while.33 = (s32[]{:T(128)}, bf16[4,512,3,64]{1,3,2,0:T(8,128)(2,1)}, f32[4,1024,3,64]{1,3,2,0:T(8,128)}, f32[4,1024,3,64]{1,3,2,0:T(8,128)}, s32[4]{0:T(128)S(1...) while((s32[]{:T(128)}, ...), condition=%wide.region_15.16_spmd, body=%wide.region_13.15_spmd.sunk | while | flops 1031043584 | bytes 59572856 | solution.py:231
  482.7 2.8 fusion.164
  498.8 2.8 fusion.164
  514.9 2.8 fusion.164
  530.9 2.8 fusion.164
  565.2 6.2 bitcast_convert_fusion
  574.9 2.9 multiply_subtract_fusion
  578.4 50.8 %reduce-scatter.19.cloned.1.call-done = bf16[96,768]{1,0:T(8,128)(2,1)} async-done(((bf16[768,768]{1,0:T(8,128)(2,1)}), bf16[96,768]{1,0:T(8,128)(2,1)}) %reduce-scatter.19.cloned.1.call-update) | async-done | bytes 147472
  637.5 31.3 %reduce-scatter.15.cloned.1.call-done = bf16[2,256,768]{2,1,0:T(8,128)(2,1)} async-done(((bf16[2,1024,768]{2,1,0:T(8,128)(2,1)}), bf16[2,256,768]{2,1,0:T(8,128)(2,1)}) %reduce-scatter.15.cloned.1.call-update) | async-done | bytes 786448 | tf_op jit(solution)/shard_map/reduce_scatter | solution.py:250
  671.3 39.7 %psum.7 = f32[12,768]{1,0:T(8,128)S(1)} all-reduce(f32[12,768]{1,0:T(8,128)S(1)} %concatenate.8), channel_id=1, replica_groups=mesh['wide'=8,'narrow'=4] {'wide','narrow'}, use_global_device_ids=true, to_apply=%region_32.33 | all-reduce | flops 9216 | bytes 73728 | tf_op jit(solution)/shard_map/psum | solution.py:288
  711.8 3.0 fusion.72
  (269 shorter events, 141.5 us)
Async XLA Ops:
  7.2 50.5 %all-gather.9.cloned.1.call-start = ((), (), s32[]{:S(2)}) async-start(), calls=%async_computation.7 | async-start | bytes 1769472 | tf_op jit(solution)/shard_map/all_gather | solution.py:83
  9.2 77.4 %all-gather.7.cloned.1.call-start = ((), (), s32[]{:S(2)}) async-start(), calls=%async_computation.6 | async-start | bytes 3932160 | tf_op jit(solution)/shard_map/all_gather | solution.py:87
  9.9 196.2 %reduce-scatter.9.cloned.1.call-start = ((), (), s32[]{:S(2)}) async-start(), calls=%async_computation.8 | async-start | bytes 7864320 | tf_op jit(solution)/shard_map/reduce_scatter | solution.py:153
  11.8 82.1 %copy-start.24 = (f32[768]{0:T(1024)}, f32[768]{0:T(1024)S(1)}, u32[]{:S(2)}) copy-start(f32[768]{0:T(1024)S(1)} %get-tuple-element.520) | copy-start | bytes 9220
  57.7 2.9 copy-start.7
  61.5 33.7 %copy-start.16 = (bf16[3,768,192]{1,2,0:T(8,128)(2,1)}, bf16[3,768,192]{1,2,0:T(8,128)(2,1)S(1)}, u32[]{:S(2)}) copy-start(bf16[3,768,192]{1,2,0:T(8,128)(2,1)S(1)} %copy.93) | copy-start | bytes 2654212
  86.6 2.8 copy-start
  139.3 8.3 %copy-start.3 = (bf16[2,1024,3,64]{1,3,2,0:T(8,128)(2,1)}, bf16[2,1024,3,64]{1,3,2,0:T(8,128)(2,1)S(1)}, u32[]{:S(2)}) copy-start(bf16[2,1024,3,64]{1,3,2,0:T(8,128)(2,1)S(1)} %get-tuple-element.774) | copy-start | bytes 2359300
  141.4 6.2 copy-start.5
  147.6 113.3 %all-gather.13.cloned.1.call-start = ((), (), s32[]{:S(2)}) async-start(), calls=%async_computation.10 | async-start | bytes 2654208 | tf_op jit(solution)/shard_map/all_gather | solution.py:84
  149.4 140.7 %all-gather.11.cloned.1.call-start = ((), (), s32[]{:S(2)}) async-start(), calls=%async_computation.9 | async-start | bytes 3932160 | tf_op jit(solution)/shard_map/all_gather | solution.py:160
  209.6 110.6 %all-gather.15.cloned.1.call-start = ((), (), s32[]{:S(2)}) async-start(), calls=%async_computation.12 | async-start | bytes 3932160 | tf_op jit(solution)/shard_map/all_gather | solution.py:88
  210.2 185.3 %reduce-scatter.13.cloned.1.call-start = ((), (), s32[]{:S(2)}) async-start(), calls=%async_computation.13 | async-start | bytes 7864320 | tf_op jit(solution)/shard_map/reduce_scatter | solution.py:185
  320.2 12.3 %copy-start.30 = (bf16[2,768,768]{2,1,0:T(8,128)(2,1)S(1)}, bf16[2,768,768]{2,1,0:T(8,128)(2,1)}, u32[]{:S(2)}) copy-start(bf16[2,768,768]{2,1,0:T(8,128)(2,1)} %all-gather.13.cloned.1.call-done) | copy-start | bytes 7077892
  337.0 99.1 %reduce-scatter.11.cloned.1.call-start = ((), (), s32[]{:S(2)}) async-start(), calls=%async_computation.11 | async-start | bytes 3932160 | tf_op jit(solution)/shard_map/reduce_scatter | solution.py:166
  343.6 92.4 %copy-start.28 = (f32[768]{0:T(1024)S(1)}, f32[768]{0:T(1024)}, u32[]{:S(2)}) copy-start(f32[768]{0:T(1024)} %get-tuple-element.525) | copy-start | bytes 9220
  343.7 126.8 %all-gather.17.cloned.1.call-start = ((), (), s32[]{:S(2)}) async-start(), calls=%async_computation.14 | async-start | bytes 3932160 | tf_op jit(solution)/shard_map/all_gather | solution.py:194
  441.8 133.1 %reduce-scatter.17.cloned.1.call-start = ((), (), s32[]{:S(2)}) async-start(), calls=%async_computation.16 | async-start | bytes 2654208 | tf_op jit(solution)/shard_map/reduce_scatter | solution.py:295
  442.9 5.7 copy-start.29
  442.9 5.7 copy-start.32
  452.9 176.3 %reduce-scatter.19.cloned.1.call-start = ((), (), s32[]{:S(2)}) async-start(), calls=%async_computation.17 | async-start | bytes 1327104
  553.5 3.6 copy-start.10
  553.6 5.5 copy-start.21
  565.1 103.7 %reduce-scatter.15.cloned.1.call-start = ((), (), s32[]{:S(2)}) async-start(), calls=%async_computation.15 | async-start | bytes 3932160 | tf_op jit(solution)/shard_map/reduce_scatter | solution.py:250
  571.4 3.5 copy-start.14
  578.2 90.6 %copy-start.25 = (f32[768]{0:T(1024)S(1)}, f32[768]{0:T(1024)}, u32[]{:S(2)}) copy-start(f32[768]{0:T(1024)} %copy-done.24) | copy-start | bytes 9220
  631.4 79.6 %copy-start.23 = (f32[12,768]{1,0:T(8,128)S(1)}, f32[12,768]{1,0:T(8,128)}, u32[]{:S(2)}) copy-start(f32[12,768]{1,0:T(8,128)} %param.25) | copy-start | bytes 110596
  631.4 79.6 %copy-start.26 = (f32[12,768]{1,0:T(8,128)S(1)}, f32[12,768]{1,0:T(8,128)}, u32[]{:S(2)}) copy-start(f32[12,768]{1,0:T(8,128)} %param.26) | copy-start | bytes 110596
  631.4 79.6 %copy-start.27 = (f32[12,768]{1,0:T(8,128)S(1)}, f32[12,768]{1,0:T(8,128)}, u32[]{:S(2)}) copy-start(f32[12,768]{1,0:T(8,128)} %param.27) | copy-start | bytes 110596
  632.6 79.2 %copy-start.2 = (f32[2,256,768]{2,1,0:T(8,128)S(1)}, f32[2,256,768]{2,1,0:T(8,128)}, u32[]{:S(2)}) copy-start(f32[2,256,768]{2,1,0:T(8,128)} %copy-done.1) | copy-start | bytes 4718596
  668.8 43.0 %copy-start.12 = (bf16[2,256,768]{2,1,0:T(8,128)(2,1)S(1)}, bf16[2,256,768]{2,1,0:T(8,128)(2,1)}, u32[]{:S(2)}) copy-start(bf16[2,256,768]{2,1,0:T(8,128)(2,1)} %reduce-scatter.15.cloned.1.call-done) | copy-start | bytes 2359300
  711.1 3.7 copy-start.22
  (20 other events, 36.1 us)
Sparse Core Ops, SparseCore 0:
  10.8 46.8 all-gather.8
  59.2 27.3 all-gather.6
  147.8 58.3 reduce-scatter.8
  209.0 51.9 all-gather.12
  263.0 27.0 all-gather.10
  291.6 28.5 all-gather.14
  337.1 58.3 reduce-scatter.12
  398.0 37.9 reduce-scatter.10
  441.9 28.5 all-gather.16
  474.2 69.1 reduce-scatter.16
  565.3 63.9 reduce-scatter.18
  631.8 36.9 reduce-scatter.14
where the time goes:
time: 732 us; the launch traced here: 722 us
  waiting for transfers between devices  409 us (56%)
  matrix products  122 us (17%)
  other arithmetic  54.4 us (7%)
  local copies, waits for them, and re-layouts  53.4 us (7%)
  blocking collectives  39.7 us (5%)
  loops' own time  27.1 us (4%)
  between operations  15.4 us (2%)
    reduce_scatter x1, waiting for transfers between devices, local(): lax.psum_scatter(out_part.reshape(sequence_count, seq_len, width), 'narro...  56.7 us
    unnamed x13, waiting for transfers between devices  52.2 us
    reduce_scatter x1, waiting for transfers between devices, local(): lax.psum_scatter(norm_two_part.reshape(sequence_count, seq_len, width), '...  51.6 us
    all_gather x1, waiting for transfers between devices, local(): lax.all_gather(mlp_w.astype(jnp.bfloat16), 'wide', axis=1, tiled=True)  50.6 us
    all_gather x1, waiting for transfers between devices, local(): lax.all_gather(attn_w.astype(jnp.bfloat16), 'wide', axis=1, tiled=True)  45.8 us
    psum x1, blocking collectives, local(): vec_grad = lax.psum(vec_local, ('wide', 'narrow'))  39.7 us
    reduce_scatter x1, waiting for transfers between devices, local(): lax.psum_scatter(down_part.reshape(sequence_count, seq_len, width).astype...  38.4 us
    reduce_scatter x1, waiting for transfers between devices, local(): lax.psum_scatter(norm_one_part.reshape(sequence_count, seq_len, width).as...  31.3 us
  transfers between devices with their start and end apart: 12, of which 11 were waited for; matrix products, arithmetic and copies ran while one was open for 20% of the time, Pallas kernels for 0%

commit v1 on v0

--- a/solution.py
+++ b/solution.py
@@ -13,6 +13,25 @@
 RATE_MATRIX = 0.04
 RATE_VECTOR = 0.3
 DECAY_MATRIX = 0.05
+
+
+def _check_things(inp, bus_axis, dim_k):
+    small, right_arr, then = (lax.axis_size(bus_axis), lax.axis_index(bus_axis), inp.shape[dim_k])
+    v_now, carry = (inp, 1)
+    while carry < small:
+        v_now = jnp.concatenate(
+            [
+                v_now,
+                lax.ppermute(
+                    v_now,
+                    axis_name=bus_axis,
+                    perm=[(ix, (ix - carry) % small) for ix in range(small)],
+                ),
+            ],
+            axis=dim_k,
+        )
+        carry = 2 * carry
+    return jnp.roll(v_now, shift=right_arr * then, axis=dim_k)
 
 
 def norm_shard_pieces(values_in, gain_vec, shift_vec):
@@ -191,9 +210,9 @@
     residual_local = own_cot + norm_backward_pass(
         second_norm_local, second_standardized_local, inv_two_own, second_norm_gain
     )
-    resid_low = lax.all_gather(
-        residual_local.astype(jnp.bfloat16), "narrow", axis=1, tiled=True
-    ).reshape(token_count, width)
+    resid_low = _check_things(residual_local.astype(jnp.bfloat16), "narrow", 1).reshape(
+        token_count, width
+    )
     grad_out_w = jnp.einsum(
         "td,tc->dc", resid_low, context_rows, preferred_element_type=jnp.float32
     )

time: 732 us -> 764 us (1.044)
  waiting for transfers between devices: 409 us -> 427 us
  local copies, waits for them, and re-layouts: 53.4 us -> 66.5 us
    ppermute x0 -> x2, waiting for transfers between devices: none -> 33.9 us  [_check_things(): lax.ppermute(v_now, axis_name=bus_axis, perm=[(ix, (ix - carry) % small)...]
    all_gather x1 -> x0, waiting for transfers between devices: 17.5 us -> none  [local(): lax.all_gather(residual_local.astype(jnp.bfloat16), 'narrow', axis=1, til...]
    unnamed x79 -> x87, local copies, waits for them, and re-layouts: 25.9 us -> 34.2 us
    unnamed x13 -> x12, waiting for transfers between devices: 52.2 us -> 53.7 us
  transfers between devices with their start and end apart: 12 -> 13, of which waited for: 11 -> 12; matrix products, arithmetic and copies ran while one was open for 20% -> 20% of each run, Pallas kernels for 0% -> 0%
where the time goes in v1:
time: 764 us; the launch traced here: 754 us
  waiting for transfers between devices  427 us (56%)
  matrix products  119 us (16%)
  local copies, waits for them, and re-layouts  66.5 us (9%)
  other arithmetic  57.1 us (7%)
  blocking collectives  39.7 us (5%)
  loops' own time  27.1 us (4%)
  between operations  15 us (2%)
    reduce_scatter x1, waiting for transfers between devices, local(): lax.psum_scatter(out_part.reshape(sequence_count, seq_len, width), 'narro...  56.7 us
    unnamed x12, waiting for transfers between devices  53.7 us
    reduce_scatter x1, waiting for transfers between devices, local(): lax.psum_scatter(norm_two_part.reshape(sequence_count, seq_len, width), '...  51.6 us
    all_gather x1, waiting for transfers between devices, local(): lax.all_gather(mlp_w.astype(jnp.bfloat16), 'wide', axis=1, tiled=True)  50.6 us
    all_gather x1, waiting for transfers between devices, local(): lax.all_gather(attn_w.astype(jnp.bfloat16), 'wide', axis=1, tiled=True)  45.8 us
    psum x1, blocking collectives, local(): vec_grad = lax.psum(vec_local, ('wide', 'narrow'))  39.7 us
    reduce_scatter x1, waiting for transfers between devices, local(): lax.psum_scatter(down_part.reshape(sequence_count, seq_len, width).astype...  38.4 us
    unnamed x87, local copies, waits for them, and re-layouts  34.2 us
  transfers between devices with their start and end apart: 13, of which 12 were waited for; matrix products, arithmetic and copies ran while one was open for 20% of the time, Pallas kernels for 0%

profile of v1, /device:TPU:0, one launch (start us, length us, event | category | flops | bytes accessed | tf_op | source)
XLA Modules:
  0.0 754.3 jit_solution(10677976137465858124)
XLA Ops:
  11.9 45.8 %all-gather.8.cloned.1.call-done = bf16[4,768,192]{2,0,1:T(4,128)(2,1)} async-done(((bf16[4,96,192]{2,0,1:T(4,128)(2,1)}), bf16[4,768,192]{2,0,1:T(4,128)(2,1)}) %all-gather.8.cloned.1.call-update) | async-done | bytes 1179664 | tf_op jit(solution)/shard_map/all_gather | solution.py:102
  61.5 25.1 %all-gather.6.cloned.1.call-done = bf16[2,1024,768]{2,1,0:T(8,128)(2,1)} async-done(((bf16[2,256,768]{2,1,0:T(8,128)(2,1)}), bf16[2,1024,768]{2,1,0:T(8,128)(2,1)}) %all-gather.6.cloned.1.call-update) | async-done | bytes 3145744 | tf_op jit(solution)/shard_map/all_gather | solution.py:106
  89.5 3.8 convert_subtract_fusion
  100.1 39.2 %while.32 = (s32[]{:T(128)}, bf16[4,512,3,64]{1,3,2,0:T(8,128)(2,1)}, f32[4,3,512]{2,1,0:T(4,128)S(1)}, s32[4]{0:T(128)S(1)}, bf16[2,1024,3,64]{1,3,2,0:T(8,128)...) while((s32[]{:T(128)}, ...), condition=%wide.region_5.6_spmd, body=%wide.region_2.5_spmd.sunk | while | flops 422148640 | bytes 22229476 | solution.py:167
  107.1 2.7 fusion.152
  126.5 2.7 fusion.152
  142.8 4.8 fusion.97
  149.5 56.7 %reduce-scatter.9.cloned.1.call-done = f32[2,256,768]{2,1,0:T(8,128)} async-done(((f32[2,1024,768]{2,1,0:T(8,128)}), f32[2,256,768]{2,1,0:T(8,128)}) %reduce-scatter.9.cloned.1.call-update) | async-done | bytes 1572880 | tf_op jit(solution)/shard_map/reduce_scatter | solution.py:172
  210.3 50.6 %all-gather.12.cloned.1.call-done = bf16[2,768,768]{2,1,0:T(8,128)(2,1)} async-done(((bf16[2,96,768]{2,1,0:T(8,128)(2,1)}), bf16[2,768,768]{2,1,0:T(8,128)(2,1)}) %all-gather.12.cloned.1.call-update) | async-done | bytes 2359312 | tf_op jit(solution)/shard_map/all_gather | solution.py:103
  261.0 29.2 %all-gather.10.cloned.1.call-done = bf16[2,1024,768]{2,1,0:T(8,128)(2,1)} async-done(((bf16[2,256,768]{2,1,0:T(8,128)(2,1)}), bf16[2,1024,768]{2,1,0:T(8,128)(2,1)}) %all-gather.10.cloned.1.call-update) | async-done | bytes 3145744 | tf_op jit(solution)/shard_map/all_gather | solution.py:179
  290.1 19.0 %multiply_convert_fusion.1 = (bf16[2048,768]{1,0:T(8,128)(2,1)}, f32[2048,768]{1,0:T(8,128)}, f32[2048,768]{1,0:T(8,128)}) fusion(f32[768]{0:T(1024)S(1)} %dynamic_slice.114, bf16[2048,768]{1,0:T(8,128)(2,1)} %bitcast.256, bf16[2,768,768]{2,1,0:T(8,128)(2,1)} %all-gather.12.cloned.1.call-done), kind=kOutput, calls=%fused_computation.73 | convolution fusion | flops 2519728128 | bytes 20057088 | tf_op jit(solution)/shard_map/dot_general | solution.py:182
  309.1 11.1 %all-gather.14.cloned.1.call-done = bf16[2,1024,768]{2,1,0:T(8,128)(2,1)} async-done(((bf16[2,256,768]{2,1,0:T(8,128)(2,1)}), bf16[2,1024,768]{2,1,0:T(8,128)(2,1)}) %all-gather.14.cloned.1.call-update) | async-done | bytes 3145744 | tf_op jit(solution)/shard_map/all_gather | solution.py:107
  320.2 10.6 %convert_reduce_fusion = (f32[768]{0:T(1024)S(1)}, bf16[2048,768]{1,0:T(8,128)(2,1)S(1)}) fusion(f32[2048,768]{1,0:T(8,128)} %get-tuple-element.506, bf16[2048,768]{1,0:T(8,128)(2,1)} %bitcast.258, bf16[2,768,768]{2,1,0:T(8,128)(2,1)} %all-gather.12.cloned.1.call-done, f32[2048,768]{1,0:T(8,128)} %get-tuple-element.532, f32[768]{0:T(1024)S(1)} %dynamic_slice.114), kind=kOutput, calls=%fused_computation.71 | convolution fusion | flops 2442657024 | bytes 20060160 | tf_op jit(solution)/shard_map/dot_general | solution.py:196
  332.5 4.5 fusion.83
  337.0 6.6 convolution_convert_fusion.1
  343.9 51.6 %reduce-scatter.13.cloned.1.call-done = f32[2,256,768]{2,1,0:T(8,128)} async-done(((f32[2,1024,768]{2,1,0:T(8,128)}), f32[2,256,768]{2,1,0:T(8,128)}) %reduce-scatter.13.cloned.1.call-update) | async-done | bytes 1572880 | tf_op jit(solution)/shard_map/reduce_scatter | solution.py:204
  397.6 38.4 %reduce-scatter.11.cloned.1.call-done = bf16[2,256,768]{2,1,0:T(8,128)(2,1)} async-done(((bf16[2,1024,768]{2,1,0:T(8,128)(2,1)}), bf16[2,256,768]{2,1,0:T(8,128)(2,1)}) %reduce-scatter.11.cloned.1.call-update) | async-done | bytes 786448 | tf_op jit(solution)/shard_map/reduce_scatter | solution.py:185
  436.0 3.6 fusion.107
  443.1 8.7 %collective-permute-done = bf16[2,256,768]{2,1,0:T(8,128)(2,1)S(1)} collective-permute-done((bf16[2,256,768]{2,1,0:T(8,128)(2,1)}, bf16[2,256,768]{2,1,0:T(8,128)(2,1)S(1)}, u32[]{:S(2)}, u32[]{:S(2)}) %collective-permute-start) | collective-permute-done | bytes 786464 | tf_op jit(solution)/shard_map/ppermute | solution.py:25
  455.7 4.9 fusion.79
  466.0 25.2 %collective-permute-done.1 = bf16[2,512,768]{2,1,0:T(8,128)(2,1)} collective-permute-done((bf16[2,512,768]{2,1,0:T(8,128)(2,1)}, bf16[2,512,768]{2,1,0:T(8,128)(2,1)}, u32[]{:S(2)}, u32[]{:S(2)}) %collective-permute-start.1) | collective-permute-done | bytes 1572896 | tf_op jit(solution)/shard_map/ppermute | solution.py:25
  507.4 64.5 %while.33 = (s32[]{:T(128)}, bf16[4,512,3,64]{1,3,2,0:T(8,128)(2,1)}, f32[4,1024,3,64]{1,3,2,0:T(8,128)}, f32[4,1024,3,64]{1,3,2,0:T(8,128)}, s32[4]{0:T(128)S(1...) while((s32[]{:T(128)}, ...), condition=%wide.region_15.16_spmd, body=%wide.region_13.15_spmd.sunk | while | flops 1031043584 | bytes 59572856 | solution.py:250
  513.8 2.8 fusion.164
  529.9 2.8 fusion.164
  545.9 2.8 fusion.164
  562.0 2.8 fusion.164
  596.2 6.2 bitcast_convert_fusion
  605.9 2.9 multiply_subtract_fusion
  609.4 52.3 %reduce-scatter.19.cloned.1.call-done = bf16[96,768]{1,0:T(8,128)(2,1)} async-done(((bf16[768,768]{1,0:T(8,128)(2,1)}), bf16[96,768]{1,0:T(8,128)(2,1)}) %reduce-scatter.19.cloned.1.call-update) | async-done | bytes 147472
  670.0 31.4 %reduce-scatter.15.cloned.1.call-done = bf16[2,256,768]{2,1,0:T(8,128)(2,1)} async-done(((bf16[2,1024,768]{2,1,0:T(8,128)(2,1)}), bf16[2,256,768]{2,1,0:T(8,128)(2,1)}) %reduce-scatter.15.cloned.1.call-update) | async-done | bytes 786448 | tf_op jit(solution)/shard_map/reduce_scatter | solution.py:269
  703.9 39.7 %psum.7 = f32[12,768]{1,0:T(8,128)S(1)} all-reduce(f32[12,768]{1,0:T(8,128)S(1)} %concatenate.20), channel_id=1, replica_groups=mesh['wide'=8,'narrow'=4] {'wide','narrow'}, use_global_device_ids=true, to_apply=%region_32.33 | all-reduce | flops 9216 | bytes 73728 | tf_op jit(solution)/shard_map/psum | solution.py:307
  744.3 3.0 fusion.72
  (281 shorter events, 159.8 us)
Async XLA Ops:
  7.2 50.5 %all-gather.8.cloned.1.call-start = ((), (), s32[]{:S(2)}) async-start(), calls=%async_computation.7 | async-start | bytes 1769472 | tf_op jit(solution)/shard_map/all_gather | solution.py:102
  9.2 77.4 %all-gather.6.cloned.1.call-start = ((), (), s32[]{:S(2)}) async-start(), calls=%async_computation.6 | async-start | bytes 3932160 | tf_op jit(solution)/shard_map/all_gather | solution.py:106
  9.9 196.2 %reduce-scatter.9.cloned.1.call-start = ((), (), s32[]{:S(2)}) async-start(), calls=%async_computation.8 | async-start | bytes 7864320 | tf_op jit(solution)/shard_map/reduce_scatter | solution.py:172
  11.8 82.1 %copy-start.25 = (f32[768]{0:T(1024)}, f32[768]{0:T(1024)S(1)}, u32[]{:S(2)}) copy-start(f32[768]{0:T(1024)S(1)} %get-tuple-element.522) | copy-start | bytes 9220
  61.5 33.7 %copy-start.17 = (bf16[3,768,192]{1,2,0:T(8,128)(2,1)}, bf16[3,768,192]{1,2,0:T(8,128)(2,1)S(1)}, u32[]{:S(2)}) copy-start(bf16[3,768,192]{1,2,0:T(8,128)(2,1)S(1)} %copy.93) | copy-start | bytes 2654212
  139.3 8.3 %copy-start.5 = (bf16[2,1024,3,64]{1,3,2,0:T(8,128)(2,1)}, bf16[2,1024,3,64]{1,3,2,0:T(8,128)(2,1)S(1)}, u32[]{:S(2)}) copy-start(bf16[2,1024,3,64]{1,3,2,0:T(8,128)(2,1)S(1)} %get-tuple-element.775) | copy-start | bytes 2359300
  141.4 6.2 copy-start.7
  147.6 113.3 %all-gather.12.cloned.1.call-start = ((), (), s32[]{:S(2)}) async-start(), calls=%async_computation.10 | async-start | bytes 2654208 | tf_op jit(solution)/shard_map/all_gather | solution.py:103
  149.4 140.7 %all-gather.10.cloned.1.call-start = ((), (), s32[]{:S(2)}) async-start(), calls=%async_computation.9 | async-start | bytes 3932160 | tf_op jit(solution)/shard_map/all_gather | solution.py:179
  209.6 110.6 %all-gather.14.cloned.1.call-start = ((), (), s32[]{:S(2)}) async-start(), calls=%async_computation.12 | async-start | bytes 3932160 | tf_op jit(solution)/shard_map/all_gather | solution.py:107
  210.2 185.3 %reduce-scatter.13.cloned.1.call-start = ((), (), s32[]{:S(2)}) async-start(), calls=%async_computation.13 | async-start | bytes 7864320 | tf_op jit(solution)/shard_map/reduce_scatter | solution.py:204
  320.2 12.3 %copy-start.32 = (bf16[2,768,768]{2,1,0:T(8,128)(2,1)S(1)}, bf16[2,768,768]{2,1,0:T(8,128)(2,1)}, u32[]{:S(2)}) copy-start(bf16[2,768,768]{2,1,0:T(8,128)(2,1)} %all-gather.12.cloned.1.call-done) | copy-start | bytes 7077892
  337.0 99.1 %reduce-scatter.11.cloned.1.call-start = ((), (), s32[]{:S(2)}) async-start(), calls=%async_computation.11 | async-start | bytes 3932160 | tf_op jit(solution)/shard_map/reduce_scatter | solution.py:185
  343.6 92.4 %copy-start.29 = (f32[768]{0:T(1024)S(1)}, f32[768]{0:T(1024)}, u32[]{:S(2)}) copy-start(f32[768]{0:T(1024)} %get-tuple-element.527) | copy-start | bytes 9220
  343.6 262.3 %reduce-scatter.17.cloned.1.call-start = ((), (), s32[]{:S(2)}) async-start(), calls=%async_computation.15 | async-start | bytes 2654208 | tf_op jit(solution)/shard_map/reduce_scatter | solution.py:314
  442.0 9.8 %collective-permute-start = (bf16[2,256,768]{2,1,0:T(8,128)(2,1)}, bf16[2,256,768]{2,1,0:T(8,128)(2,1)S(1)}, u32[]{:S(2)}, u32[]{:S(2)}) collective-permute-start(bf16[2,256,768]{2,1,0:T(8,128)(2,1)} %get-tuple-element.504), channel_id=1, source_target_pairs={{0,3},{1,0},{2,1},{3,2},{4,7},{5,4},{6,5},{7,6},{8,11},{9,8},{10,9... | collective-permute-start | bytes 2359304 | tf_op jit(solution)/shard_map/ppermute | solution.py:25
  442.0 13.7 %copy-start.31 = (bf16[2,1024,768]{2,1,0:T(8,128)(2,1)S(1)}, bf16[2,1024,768]{2,1,0:T(8,128)(2,1)}, u32[]{:S(2)}) copy-start(bf16[2,1024,768]{2,1,0:T(8,128)(2,1)} %all-gather.14.cloned.1.call-done) | copy-start | bytes 9437188
  454.2 6.4 copy-start.30
  454.2 6.4 copy-start.34
  454.2 37.0 %collective-permute-start.1 = (bf16[2,512,768]{2,1,0:T(8,128)(2,1)}, bf16[2,512,768]{2,1,0:T(8,128)(2,1)}, u32[]{:S(2)}, u32[]{:S(2)}) collective-permute-start(bf16[2,512,768]{2,1,0:T(8,128)(2,1)} %pad_maximum_fusion.1), channel_id=1, source_target_pairs={{0,2},{1,3},{2,0},{3,1},{4,6},{5,7},{6,4},{7,5},{8,10},{9,11},{10,... | collective-permute-start | bytes 4718600 | tf_op jit(solution)/shard_map/ppermute | solution.py:25
  465.0 196.7 %reduce-scatter.19.cloned.1.call-start = ((), (), s32[]{:S(2)}) async-start(), calls=%async_computation.16 | async-start | bytes 1327104
  584.5 3.6 copy-start.12
  584.5 5.5 copy-start.22
  596.1 105.3 %reduce-scatter.15.cloned.1.call-start = ((), (), s32[]{:S(2)}) async-start(), calls=%async_computation.14 | async-start | bytes 3932160 | tf_op jit(solution)/shard_map/reduce_scatter | solution.py:269
  602.4 3.5 copy-start.15
  609.2 92.2 %copy-start.26 = (f32[768]{0:T(1024)S(1)}, f32[768]{0:T(1024)}, u32[]{:S(2)}) copy-start(f32[768]{0:T(1024)} %copy-done.25) | copy-start | bytes 9220
  663.9 79.7 %copy-start.24 = (f32[12,768]{1,0:T(8,128)S(1)}, f32[12,768]{1,0:T(8,128)}, u32[]{:S(2)}) copy-start(f32[12,768]{1,0:T(8,128)} %param.25) | copy-start | bytes 110596
  663.9 79.7 %copy-start.27 = (f32[12,768]{1,0:T(8,128)S(1)}, f32[12,768]{1,0:T(8,128)}, u32[]{:S(2)}) copy-start(f32[12,768]{1,0:T(8,128)} %param.26) | copy-start | bytes 110596
  663.9 79.7 %copy-start.28 = (f32[12,768]{1,0:T(8,128)S(1)}, f32[12,768]{1,0:T(8,128)}, u32[]{:S(2)}) copy-start(f32[12,768]{1,0:T(8,128)} %param.27) | copy-start | bytes 110596
  665.1 79.3 %copy-start.2 = (f32[2,256,768]{2,1,0:T(8,128)S(1)}, f32[2,256,768]{2,1,0:T(8,128)}, u32[]{:S(2)}) copy-start(f32[2,256,768]{2,1,0:T(8,128)} %copy-done.1) | copy-start | bytes 4718596
  701.4 43.0 %copy-start.13 = (bf16[2,256,768]{2,1,0:T(8,128)(2,1)S(1)}, bf16[2,256,768]{2,1,0:T(8,128)(2,1)}, u32[]{:S(2)}) copy-start(bf16[2,256,768]{2,1,0:T(8,128)(2,1)} %reduce-scatter.15.cloned.1.call-done) | copy-start | bytes 2359300
  743.6 3.7 copy-start.23
  (23 other events, 43.7 us)
Sparse Core Ops, SparseCore 0:
  10.8 46.8 all-gather.7
  59.2 27.3 all-gather.5
  147.8 58.3 reduce-scatter.8
  209.0 51.9 all-gather.11
  263.0 27.0 all-gather.9
  291.6 28.5 all-gather.13
  337.1 58.3 reduce-scatter.12
  398.0 37.9 reduce-scatter.10
  465.1 70.1 reduce-scatter.16
  596.2 65.4 reduce-scatter.18
  664.4 36.9 reduce-scatter.14
